TPU v7x, 32 devices: a whole 2x2x4 slice. The times are simulated.
32 devices in a mesh: section: 2 (over core), tile: 4 (over z), mem: 4 (over y, x).
Axes of the slice: x: 2, y: 2, z: 4, core: 2. Of those that a mesh axis runs over, the one named last changes fastest.
Arguments:
- state: float32 [32, 16, 64, 128], P(('section', 'mem'), None, 'tile'), may hold values from -6 to 6
- speed_x: float32 [16, 64, 128], P(None, 'tile'), may hold values from -0.35 to 0.35
- speed_y: float32 [16, 64, 128], P(None, 'tile'), may hold values from -0.35 to 0.35
- diffuse: float32 [64, 128], P('tile'), may hold values from 0.02 to 0.07
- obs_cell: int32 [4096], P('tile'), may hold values from 0 to 32767, as said below
- obs_value: float32 [4096], P('tile'), may hold values from -6 to 6
- obs_errinv: float32 [4096], P('tile'), may hold values from 0.05 to 0.5
- obs_list: int32 [32, 64, 256], P('tile'), may hold values from 0 to 3071, as said below
- obs_count: int32 [32, 64], P('tile'), may hold values from 1 to 256, as said below
Outputs:
- analysis: float32 [32, 16, 64, 128], P(('section', 'mem'), None, 'tile')
Inputs may be any that keep to these rules, and one draw needn't show every extreme that they name: `obs_cell`: level * 16 * 128 + x * 128 + y of the observation inside its tile. `obs_list`: each row holds 256 different window indices k * 1024 + i, meaning observation i of the tile k - 1 places after the domain's tile; they list window columns nearest first by horizontal distance to the domain's centre; columns beyond 4 * 4 cells and columns outside the grid count as equally far, and ties go by increasing window index, so list tails near the grid's ends may name columns outside it. Only the first obs_count slots of a domain's list are used; away from a few domains, obs_count does not exceed the number of window observations within 2.5 * 4 cells of the centre.
All inputs are finite; a program needn't handle non-finite values.
Results may differ from a plain program's by a relative error of at most 0.0003.
Values sent between devices are 32-bit elements; how exact they have to be, the bound alone decides.
No kernel may reach another device: no remote copies, remote signals or barrier semaphores. Data moves between devices by JAX's collectives and lax.ppermute only.
A program may use at most 64 MiB of HBM per device.

v0:
```python
import jax
import jax.numpy as jnp
from jax import lax
from jax.sharding import PartitionSpec as P

STEPS = 4
DB = 2
LOC = 4


def padded_2(block, sides, width):
    for axis, dim in sides:
        count = lax.axis_size(axis)
        forward = [(i, i + 1) for i in range(count - 1)]
        backward = [(target, source) for source, target in forward]
        low = lax.ppermute(
            lax.slice_in_dim(block, block.shape[dim] - width, None, axis=dim), axis, forward
        )
        high = lax.ppermute(lax.slice_in_dim(block, 0, width, axis=dim), axis, backward)
        block = jnp.concatenate([low, block, high], axis=dim)
    return block


def advance(center, left_x, right_x, speed_x, speed_y, diffuse):
    zero_col = jnp.zeros_like(center[..., :1])
    lower_y = jnp.concatenate([zero_col, center[..., :-1]], axis=-1)
    upper_y = jnp.concatenate([center[..., 1:], zero_col], axis=-1)
    return (
        center
        - jnp.maximum(speed_x, 0.0) * (center - left_x)
        - jnp.minimum(speed_x, 0.0) * (right_x - center)
        - jnp.maximum(speed_y, 0.0) * (center - lower_y)
        - jnp.minimum(speed_y, 0.0) * (upper_y - center)
        + diffuse * (left_x + right_x + lower_y + upper_y - 4.0 * center)
    )


def analyze(state_fields, window, lists, counts, x_anchor):
    members = state_fields.shape[0]
    levels = state_fields.shape[1]
    rows_d = lists.shape[0]
    cols_d = lists.shape[1]
    slots = lists.shape[2]
    flat_lists = lists.reshape(rows_d * cols_d, slots)
    chosen = window[:, flat_lists]
    observed_ensemble = chosen[:members]
    ens_mean = jnp.mean(observed_ensemble, axis=0)
    perturb = observed_ensemble - ens_mean
    centre_x = x_anchor + (jnp.arange(rows_d) * DB).astype(jnp.float32) + 0.5 * (DB - 1)
    centre_y = (jnp.arange(cols_d) * DB).astype(jnp.float32) + 0.5 * (DB - 1)
    centre_x = jnp.broadcast_to(centre_x[:, None], (rows_d, cols_d)).reshape(-1)
    centre_y = centre_y[None, :].reshape(-1)
    dist_sq = (chosen[members] - centre_x[:, None]) ** 2 + (
        chosen[members + 1] - centre_y[:, None]
    ) ** 2
    live = (jnp.arange(slots)[None, :] < counts.reshape(-1)[:, None]).astype(jnp.float32)
    weight = chosen[members + 3] * jnp.exp(-dist_sq / (2.0 * LOC * LOC)) * live
    weighted = perturb * weight
    identity = jnp.eye(members, dtype=jnp.float32)
    gram = (
        jnp.einsum("knm,jnm->nkj", weighted, perturb, precision=lax.Precision.HIGHEST)
        + (members - 1.0) * identity
    )
    forcing = jnp.einsum(
        "knm,nm->nk", weighted, chosen[members + 2] - ens_mean, precision=lax.Precision.HIGHEST
    )
    factor = jnp.linalg.cholesky(gram)
    mean_w = jax.scipy.linalg.cho_solve((factor, True), forcing[..., None])[..., 0]
    inverse_l = jax.scipy.linalg.solve_triangular(
        factor, jnp.broadcast_to(identity, gram.shape), lower=True
    )
    transform = jnp.sqrt(members - 1.0) * jnp.swapaxes(inverse_l, 1, 2) + mean_w[:, :, None]
    blocks = state_fields.reshape(members, levels, rows_d, DB, cols_d, DB)
    field_mean = jnp.mean(blocks, axis=0)
    anomaly = blocks - field_mean
    trans_grid = transform.reshape(rows_d, cols_d, members, members)
    result = field_mean + jnp.einsum(
        "jlaxcy,acjk->klaxcy", anomaly, trans_grid, precision=lax.Precision.HIGHEST
    )
    return result.reshape(state_fields.shape)


def local(state, speed_x, speed_y, diffuse, obs_cell, obs_value, obs_errinv, obs_list, obs_count):
    memb_dev = state.shape[0]
    width_x = state.shape[2]
    width_y = state.shape[3]
    groups = lax.axis_size(("section", "mem"))
    tile_index = lax.axis_index("tile")
    group_idx = lax.axis_index(("section", "mem"))
    current = state
    for step_idx in range(STEPS):
        padded = padded_2(current, (("tile", 2),), 1)
        current = advance(current, padded[:, :, :-2], padded[:, :, 2:], speed_x, speed_y, diffuse)
    received = lax.all_to_all(current, ("section", "mem"), split_axis=2, concat_axis=0, tiled=True)
    own_ens = current.reshape(memb_dev, -1)[:, obs_cell]
    all_ens = lax.all_gather(own_ens, ("section", "mem"), axis=0, tiled=True)
    global_x = (tile_index * width_x + obs_cell // width_y % width_x).astype(jnp.float32)
    local_y = (obs_cell % width_y).astype(jnp.float32)
    rows = jnp.concatenate(
        [all_ens, global_x[None], local_y[None], obs_value[None], obs_errinv[None]], axis=0
    )
    window = padded_2(rows, (("tile", 1),), rows.shape[1])
    share = width_x // groups
    lists = lax.dynamic_slice_in_dim(obs_list, group_idx * (share // DB), share // DB, 0)
    counts = lax.dynamic_slice_in_dim(obs_count, group_idx * (share // DB), share // DB, 0)
    x_anchor = (tile_index * width_x + group_idx * share).astype(jnp.float32)
    analysed = analyze(received, window, lists, counts, x_anchor)
    return lax.all_to_all(analysed, ("section", "mem"), split_axis=0, concat_axis=2, tiled=True)


def solution(mesh):
    placed = (
        P(("section", "mem"), None, "tile", None),
        P(None, "tile", None),
        P(None, "tile", None),
        P("tile", None),
        P("tile"),
        P("tile"),
        P("tile"),
        P("tile", None, None),
        P("tile", None),
    )
    return jax.shard_map(
        local,
        mesh=mesh,
        in_specs=placed,
        out_specs=P(("section", "mem"), None, "tile", None),
        check_vma=False,
    )
```

profile of v0, /device:TPU:0, one launch (start us, length us, event | category | flops | bytes accessed | tf_op | source)
XLA Modules:
  0.0 398.0 jit_solution(16777165683892580025)
XLA Ops:
  0.0 1.3 copy.55
  1.3 0.0 copy-start.3
  1.3 5.0 %collective-permute-start = (f32[4,16,1,128]{3,1,0,2:T(8,128)S(1)}, f32[4,16,1,128]{3,1,0,2:T(8,128)S(1)}, u32[]{:S(2)}, u32[]{:S(2)}) collective-permute-start(f32[4,16,1,128]{3,1,0,2:T(8,128)S(1)} %get-tuple-element.21), channel_id=1, source_target_pairs={{0,4},{4,8},{8,12},{1,5},{5,9},{9,13},{2,6},{6,10},{10,14},{3,7},{... | collective-permute-start | bytes 98312 | tf_op jit(solution)/shard_map/ppermute | solution.py:16
  6.3 1.3 collective-permute-start.1
  7.6 0.2 fusion.99
  7.9 0.9 fusion.76
  9.1 0.0 collective-permute-done
  9.1 3.0 collective-permute-done.1
  12.1 0.4 fusion.67
  12.5 3.5 collective-permute-start.2
  16.0 1.3 collective-permute-start.3
  17.3 0.2 fusion.97
  17.5 0.1 collective-permute-done.2
  17.6 4.2 %collective-permute-done.3 = f32[4,16,1,128]{3,1,0,2:T(8,128)S(1)} collective-permute-done((f32[4,16,1,128]{3,1,0,2:T(8,128)S(1)}, f32[4,16,1,128]{3,1,0,2:T(8,128)S(1)}, u32[]{:S(2)}, u32[]{:S(2)}) %collective-permute-start.3) | collective-permute-done | bytes 32800 | tf_op jit(solution)/shard_map/ppermute | solution.py:19
  21.8 0.4 fusion.53
  22.3 3.5 collective-permute-start.4
  25.8 1.3 collective-permute-start.5
  27.1 0.2 fusion.95
  27.3 0.1 collective-permute-done.4
  27.3 4.2 %collective-permute-done.5 = f32[4,16,1,128]{3,1,0,2:T(8,128)S(1)} collective-permute-done((f32[4,16,1,128]{3,1,0,2:T(8,128)S(1)}, f32[4,16,1,128]{3,1,0,2:T(8,128)S(1)}, u32[]{:S(2)}, u32[]{:S(2)}) %collective-permute-start.5) | collective-permute-done | bytes 32800 | tf_op jit(solution)/shard_map/ppermute | solution.py:19
  31.6 0.4 fusion.39
  32.0 1.9 collective-permute-start.6
  33.9 1.3 collective-permute-start.7
  35.2 0.2 fusion.93
  35.5 0.1 collective-permute-done.6
  35.5 4.2 %collective-permute-done.7 = f32[4,16,1,128]{3,1,0,2:T(8,128)S(1)} collective-permute-done((f32[4,16,1,128]{3,1,0,2:T(8,128)S(1)}, f32[4,16,1,128]{3,1,0,2:T(8,128)S(1)}, u32[]{:S(2)}, u32[]{:S(2)}) %collective-permute-start.7) | collective-permute-done | bytes 32800 | tf_op jit(solution)/shard_map/ppermute | solution.py:19
  39.8 1.2 fusion.25
  41.0 9.6 %copy.70 = f32[4,16,16,128]{0,3,2,1:T(8,128)} copy(f32[4,16,16,128]{3,1,0,2:T(8,128)} %fusion.25) | data formatting | bytes 1048576 | tf_op jit(solution)/shard_map/add | solution.py:29
  50.6 8.6 %gather_fusion = f32[1024,4]{1,0:T(8,128)S(1)} fusion(f32[4,32768]{0,1:T(8,128)} %bitcast.83, s32[1024]{0:T(1024)S(1)} %get-tuple-element.30), kind=kCustom, calls=%fused_computation | custom fusion | bytes 36864 | tf_op jit(solution)/shard_map/gather | solution.py:95
  59.2 0.2 copy.71
  59.4 23.5 %all-gather.1 = f32[8,4,1024]{2,1,0:T(4,128)S(1)} all-gather(f32[1,4,1024]{2,1,0:T(4,128)S(1)} %copy.71), channel_id=2, replica_groups=mesh['section'=2,'tile'=4,'mem'=4] {'section','mem'}, dimensions={0}, use_global_device_ids=true | all-gather | bytes 147456 | tf_op jit(solution)/shard_map/all_gather | solution.py:96
  83.1 1.9 collective-permute-start.8
  85.0 1.3 collective-permute-start.9
  86.3 0.1 copy.69
  86.4 3.7 all-to-all-start
  90.1 2.4 collective-permute-done.9
  92.5 0.5 copy.72
  93.0 54.4 %gather_fusion.1 = f32[16384,36]{1,0:T(8,128)} fusion(f32[36,3072]{0,1:T(8,128)S(1)} %copy.72, s32[16384]{0:T(1024)S(1)} %broadcast_clamp_fusion), kind=kCustom, calls=%fused_computation.1 | custom fusion | bytes 4784128 | tf_op jit(solution)/shard_map/gather | solution.py:45
  147.4 5.3 %copy.73 = f32[64,256,36]{1,2,0:T(8,128)S(1)} copy(f32[64,256,36]{2,1,0:T(8,128)} %bitcast.85) | data formatting | bytes 4718592 | tf_op jit(solution)/shard_map/gather | solution.py:45
  152.7 0.3 slice_reduce_fusion
  153.0 0.4 fusion.92
  153.4 3.2 fusion.4
  156.6 2.0 fusion.10
  158.6 1.6 copy.74
  160.3 1.2 fusion.14
  161.5 188.1 %custom-call.14 = f32[64,32,32]{2,1,0:T(8,128)S(1)} custom-call(f32[64,32,32]{2,1,0:T(8,128)} %fusion.14), custom_call_target="Cholesky" | custom-call | tf_op jit(solution)/shard_map/jit(cholesky)/cholesky | solution.py:67
  349.7 0.7 copy.75
  350.4 0.2 select_reduce_fusion
  350.6 0.2 select_bitcast_fusion
  350.8 12.5 %custom-call.15 = f32[64,1,32,32]{0,2,3,1:T(8,128)S(1)} custom-call(f32[64,1,32,32]{0,3,2,1:T(8,128)S(1)} %select_bitcast_fusion), custom_call_target="InvertDiagBlocksLowerTriangular" | custom-call | tf_op jit(solution)/shard_map/jit(_solve_triangular)/vmap()/triangular_solve | solution.py:69
  363.3 0.9 copy.87
  364.2 1.0 convolution_bitcast_fusion
  365.3 1.7 fusion.101
  367.0 1.1 fusion.9
  368.1 0.0 all-to-all-done
  368.1 2.8 copy.67
  371.0 2.7 bitcast_reduce_fusion
  373.7 0.7 copy-done.1
  374.4 0.6 broadcast_subtract_fusion
  375.0 8.7 %bitcast_add_fusion = f32[32,16,1,2,64,2]{0,1,5,3,4,2:T(8,128)S(1)} fusion(f32[64,32,32,1,1]{2,1,4,3,0:T(8,128)S(1)} %fusion.9, f32[32,16,2,64,2]{1,4,3,2,0:T(2,128)S(1)} %bitcast.84, f32[16,2,64,2]{0,3,2,1:T(2,128)S(1)} %bitcast.91), kind=kOutput, calls=%fused_computation.9 | convolution fusion | flops 50462720 | bytes 1327104 | tf_op jit(solution)/shard_map/jlaxcy,acjk->klaxcy/dot_general | solution.py:77
  383.7 0.2 copy.79
  383.9 1.1 copy.80
  385.0 12.0 %all_to_all.33 = f32[32,16,2,128]{3,1,2,0:T(8,128)S(1)} all-to-all(f32[32,16,2,128]{3,1,2,0:T(8,128)S(1)} %copy.80), channel_id=1, replica_groups=mesh['section'=2,'tile'=4,'mem'=4] {'section','mem'}, dimensions={0} | all-to-all | bytes 1048576 | tf_op jit(solution)/shard_map/all_to_all | solution.py:108
  397.0 1.0 copy.82
  (44 shorter events, 0.6 us)
Async XLA Ops:
  0.0 86.3 %copy-start = (s32[8,64]{1,0:T(8,128)S(1)}, s32[8,64]{1,0:T(8,128)}, u32[]{:S(2)}) copy-start(s32[8,64]{1,0:T(8,128)} %param.17) | copy-start | bytes 6148
  0.0 7.8 %copy-start.4 = (f32[16,16,128]{2,1,0:T(8,128)S(1)}, f32[16,16,128]{2,1,0:T(8,128)}, u32[]{:S(2)}) copy-start(f32[16,16,128]{2,1,0:T(8,128)} %param.10) | copy-start | bytes 393220
  0.0 7.9 %copy-start.5 = (f32[16,16,128]{2,1,0:T(8,128)S(1)}, f32[16,16,128]{2,1,0:T(8,128)}, u32[]{:S(2)}) copy-start(f32[16,16,128]{2,1,0:T(8,128)} %param.11) | copy-start | bytes 393220
  0.0 8.8 %copy-start.8 = (s32[1024]{0:T(1024)S(1)}, s32[1024]{0:T(1024)}, u32[]{:S(2)}) copy-start(s32[1024]{0:T(1024)} %param.13) | copy-start | bytes 12292
  1.3 10.8 %copy-start.3 = (f32[16,128]{1,0:T(8,128)S(1)}, f32[16,128]{1,0:T(8,128)}, u32[]{:S(2)}) copy-start(f32[16,128]{1,0:T(8,128)} %param.12) | copy-start | bytes 24580
  1.3 7.8 %collective-permute-start = (f32[4,16,1,128]{3,1,0,2:T(8,128)S(1)}, f32[4,16,1,128]{3,1,0,2:T(8,128)S(1)}, u32[]{:S(2)}, u32[]{:S(2)}) collective-permute-start(f32[4,16,1,128]{3,1,0,2:T(8,128)S(1)} %get-tuple-element.21), channel_id=1, source_target_pairs={{0,4},{4,8},{8,12},{1,5},{5,9},{9,13},{2,6},{6,10},{10,14},{3,7},{... | collective-permute-start | bytes 98312 | tf_op jit(solution)/shard_map/ppermute | solution.py:16
  6.3 5.8 %collective-permute-start.1 = (f32[4,16,1,128]{3,1,0,2:T(8,128)S(1)}, f32[4,16,1,128]{3,1,0,2:T(8,128)S(1)}, u32[]{:S(2)}, u32[]{:S(2)}) collective-permute-start(f32[4,16,1,128]{3,1,0,2:T(8,128)S(1)} %get-tuple-element.22), channel_id=1, source_target_pairs={{4,0},{8,4},{12,8},{5,1},{9,5},{13,9},{6,2},{10,6},{14,10},{7,3},{... | collective-permute-start | bytes 98312 | tf_op jit(solution)/shard_map/ppermute | solution.py:19
  12.5 5.1 %collective-permute-start.2 = (f32[4,16,1,128]{3,1,0,2:T(8,128)S(1)}, f32[4,16,1,128]{3,1,0,2:T(8,128)S(1)}, u32[]{:S(2)}, u32[]{:S(2)}) collective-permute-start(f32[4,16,1,128]{3,1,0,2:T(8,128)S(1)} %get-tuple-element.17), channel_id=1, source_target_pairs={{0,4},{4,8},{8,12},{1,5},{5,9},{9,13},{2,6},{6,10},{10,14},{3,7},{... | collective-permute-start | bytes 98312 | tf_op jit(solution)/shard_map/ppermute | solution.py:16
  16.0 5.8 %collective-permute-start.3 = (f32[4,16,1,128]{3,1,0,2:T(8,128)S(1)}, f32[4,16,1,128]{3,1,0,2:T(8,128)S(1)}, u32[]{:S(2)}, u32[]{:S(2)}) collective-permute-start(f32[4,16,1,128]{3,1,0,2:T(8,128)S(1)} %get-tuple-element.18), channel_id=1, source_target_pairs={{4,0},{8,4},{12,8},{5,1},{9,5},{13,9},{6,2},{10,6},{14,10},{7,3},{... | collective-permute-start | bytes 98312 | tf_op jit(solution)/shard_map/ppermute | solution.py:19
  22.3 5.1 %collective-permute-start.4 = (f32[4,16,1,128]{3,1,0,2:T(8,128)S(1)}, f32[4,16,1,128]{3,1,0,2:T(8,128)S(1)}, u32[]{:S(2)}, u32[]{:S(2)}) collective-permute-start(f32[4,16,1,128]{3,1,0,2:T(8,128)S(1)} %get-tuple-element.13), channel_id=1, source_target_pairs={{0,4},{4,8},{8,12},{1,5},{5,9},{9,13},{2,6},{6,10},{10,14},{3,7},{... | collective-permute-start | bytes 98312 | tf_op jit(solution)/shard_map/ppermute | solution.py:16
  25.8 5.8 %collective-permute-start.5 = (f32[4,16,1,128]{3,1,0,2:T(8,128)S(1)}, f32[4,16,1,128]{3,1,0,2:T(8,128)S(1)}, u32[]{:S(2)}, u32[]{:S(2)}) collective-permute-start(f32[4,16,1,128]{3,1,0,2:T(8,128)S(1)} %get-tuple-element.14), channel_id=1, source_target_pairs={{4,0},{8,4},{12,8},{5,1},{9,5},{13,9},{6,2},{10,6},{14,10},{7,3},{... | collective-permute-start | bytes 98312 | tf_op jit(solution)/shard_map/ppermute | solution.py:19
  32.0 3.5 collective-permute-start.6
  33.9 5.8 %collective-permute-start.7 = (f32[4,16,1,128]{3,1,0,2:T(8,128)S(1)}, f32[4,16,1,128]{3,1,0,2:T(8,128)S(1)}, u32[]{:S(2)}, u32[]{:S(2)}) collective-permute-start(f32[4,16,1,128]{3,1,0,2:T(8,128)S(1)} %get-tuple-element.10), channel_id=1, source_target_pairs={{4,0},{8,4},{12,8},{5,1},{9,5},{13,9},{6,2},{10,6},{14,10},{7,3},{... | collective-permute-start | bytes 98312 | tf_op jit(solution)/shard_map/ppermute | solution.py:19
  41.0 42.0 %copy-start.6 = (f32[1024]{0:T(1024)S(1)}, f32[1024]{0:T(1024)}, u32[]{:S(2)}) copy-start(f32[1024]{0:T(1024)} %param.14) | copy-start | bytes 12292
  41.0 42.0 %copy-start.7 = (f32[1024]{0:T(1024)S(1)}, f32[1024]{0:T(1024)}, u32[]{:S(2)}) copy-start(f32[1024]{0:T(1024)} %param.15) | copy-start | bytes 12292
  83.1 7.1 %collective-permute-start.8 = (f32[36,1024]{1,0:T(8,128)S(1)}, f32[36,1024]{1,0:T(8,128)S(1)}, u32[]{:S(2)}, u32[]{:S(2)}) collective-permute-start(f32[36,1024]{1,0:T(8,128)S(1)} %concatenate.74), channel_id=1, source_target_pairs={{0,4},{4,8},{8,12},{1,5},{5,9},{9,13},{2,6},{6,10},{10,14},{3,7},{... | collective-permute-start | bytes 442376 | tf_op jit(solution)/shard_map/ppermute | solution.py:16
  85.0 7.5 %collective-permute-start.9 = (f32[36,1024]{1,0:T(8,128)S(1)}, f32[36,1024]{1,0:T(8,128)S(1)}, u32[]{:S(2)}, u32[]{:S(2)}) collective-permute-start(f32[36,1024]{1,0:T(8,128)S(1)} %concatenate.74), channel_id=1, source_target_pairs={{4,0},{8,4},{12,8},{5,1},{9,5},{13,9},{6,2},{10,6},{14,10},{7,3},{... | collective-permute-start | bytes 442376 | tf_op jit(solution)/shard_map/ppermute | solution.py:19
  86.4 281.7 %all-to-all-start = ((f32[4,16,16,128]{3,1,0,2:T(8,128)}), f32[4,16,16,128]{3,1,0,2:T(8,128)S(1)}, u32[]{:S(2)}, u32[]{:S(2)}) async-start(f32[4,16,16,128]{3,1,0,2:T(8,128)} %fusion.25), calls=%async_computation | async-start | bytes 1048576 | tf_op jit(solution)/shard_map/all_to_all | solution.py:94
  158.6 1.7 copy-start.2
  371.0 3.4 copy-start.1
where the time goes:
time: 399 us; the launch traced here: 398 us
  other arithmetic  210 us (53%)
  local copies, waits for them, and re-layouts  90.2 us (23%)
  blocking collectives  35.5 us (9%)
  starting transfers between devices  25.9 us (6%)
  waiting for transfers between devices  18.3 us (5%)
  matrix products  17.8 us (4%)
    another operation x3, other arithmetic, analyze(): factor = jnp.linalg.cholesky(gram)  188 us
    gather x2, local copies, waits for them, and re-layouts, analyze(): chosen = window[:, flat_lists]  59.7 us
    all_gather x1, blocking collectives, local(): all_ens = lax.all_gather(own_ens, ('section', 'mem'), axis=0, tiled=True)  23.5 us
    ppermute x5, waiting for transfers between devices, padded_2(): lax.ppermute(lax.slice_in_dim(block, 0, width, axis=dim), axis, backward)  18.1 us
    ppermute x5, starting transfers between devices, padded_2(): lax.ppermute(lax.slice_in_dim(block, block.shape[dim] - width, None, axis...  15.8 us
    another operation x3, other arithmetic, analyze(): jax.scipy.linalg.solve_triangular(factor, jnp.broadcast_to(identity, gram...  12.7 us
    all_to_all x1, blocking collectives, local(): lax.all_to_all(analysed, ('section', 'mem'), split_axis=0, concat_axis=2,...  12 us
    add x1, local copies, waits for them, and re-layouts, advance(): center - jnp.maximum(speed_x, 0.0) * (center - left_x)  9.64 us
  transfers between devices with their start and end apart: 11, of which 8 were waited for; matrix products, arithmetic and copies ran while one was open for 70% of the time, Pallas kernels for 0%

commit v1 on v0

v1 whole, which is shorter than its diff:
```python
import functools

import jax
import jax.numpy as jnp
from jax import lax
from jax.experimental import pallas as pl
from jax.experimental.pallas import tpu as pltpu
from jax.sharding import PartitionSpec as P

STEPS = 4
DB = 2
LOC = 4
LANES = 128
SUB = 8
GROUP = ("section", "mem")
F32 = jnp.float32
BF16 = jnp.bfloat16


def split_2(value):
    high = value.astype(BF16)
    return high, (value - high.astype(F32)).astype(BF16)


def pack_kernel(state_ref, sx_ref, sy_ref, diff_ref, low_ref, high_ref):
    fields, width_x, _ = state_ref.shape
    levels = sx_ref.shape[0]
    for out_ref, start in ((low_ref, 0), (high_ref, width_x - STEPS)):
        rows = pl.ds(start, STEPS)
        for i in range(fields):
            out_ref[pl.ds(i * STEPS, STEPS), :] = state_ref[i, rows, :]
        for i in range(levels):
            out_ref[pl.ds((fields + i) * STEPS, STEPS), :] = sx_ref[i, rows, :]
            out_ref[pl.ds((fields + levels + i) * STEPS, STEPS), :] = sy_ref[i, rows, :]
        out_ref[pl.ds((fields + 2 * levels) * STEPS, STEPS), :] = diff_ref[rows, :]


def pack(state, speed_x, speed_y, diffuse):
    memb_dev, levels, width_x, width_y = state.shape
    fields = memb_dev * levels
    rows = -(-(fields + 2 * levels + 1) * STEPS // SUB) * SUB
    return pl.pallas_call(
        pack_kernel,
        out_shape=[jax.ShapeDtypeStruct((rows, width_y), F32)] * 2,
        name="pack",
    )(state.reshape(fields, width_x, width_y), speed_x, speed_y, diffuse)


def forecast_kernel(
    share, state_ref, low_ref, high_ref, sx_ref, sy_ref, diff_ref, cell_ref, fc_ref, obs_ref, ext_ref, all_ref
):
    fields, width_x, width_y = state_ref.shape
    levels = sx_ref.shape[0]
    memb_dev = fields // levels
    wide = width_x + 2 * STEPS
    inner = pl.ds(STEPS, width_x)

    def widen(slot, own):
        ext_ref[slot, 0:STEPS, :] = low_ref[pl.ds(slot * STEPS, STEPS), :]
        ext_ref[slot, STEPS + width_x : wide, :] = high_ref[pl.ds(slot * STEPS, STEPS), :]
        ext_ref[slot, inner, :] = own

    for i in range(fields):
        widen(i, state_ref[i])
    for i in range(levels):
        widen(fields + i, sx_ref[i])
        widen(fields + levels + i, sy_ref[i])
    widen(fields + 2 * levels, diff_ref[...])

    lane = lax.broadcasted_iota(jnp.int32, (wide, width_y), 1)

    @pl.loop(0, levels)
    def _(level):
        diff = ext_ref[fields + 2 * levels]
        sx = ext_ref[fields + level]
        sy = ext_ref[fields + levels + level]
        from_low = jnp.maximum(sx, 0.0) + diff
        from_high = diff - jnp.minimum(sx, 0.0)
        y_low = jnp.maximum(sy, 0.0) + diff
        y_high = diff - jnp.minimum(sy, 0.0)
        keep = 1.0 - (from_low + from_high + y_low + y_high)
        y_low = jnp.where(lane == 0, 0.0, y_low)
        y_high = jnp.where(lane == width_y - 1, 0.0, y_high)
        for member in range(memb_dev):
            q = ext_ref[member * levels + level]
            for _ in range(STEPS):
                q = (
                    keep * q
                    + from_low * pltpu.roll(q, 1, 0)
                    + from_high * pltpu.roll(q, wide - 1, 0)
                    + y_low * pltpu.roll(q, 1, 1)
                    + y_high * pltpu.roll(q, width_y - 1, 1)
                )
            all_ref[member, pl.ds(level * width_x, width_x), :] = q[STEPS : STEPS + width_x, :]

    for group in range(width_x // share):
        for member in range(memb_dev):
            for row in range(share):
                fc_ref[group, member, pl.ds(row * levels, levels), :] = all_ref[
                    member, pl.ds(group * share + row, levels, stride=width_x), :
                ]

    cell = cell_ref[...]
    obs = cell.shape[1]
    cell_row = cell // width_y
    cell_y = cell - cell_row * width_y
    rows = levels * width_x
    pick = (lax.broadcasted_iota(jnp.int32, (rows, obs), 0) == cell_row).astype(F32).astype(BF16)
    pick_y = lax.broadcasted_iota(jnp.int32, (width_y, obs), 0) == cell_y
    dims = (((0,), (0,)), ((), ()))
    for member in range(memb_dev):
        high, low = split_2(all_ref[member])
        found = lax.dot_general(high, pick, dims, preferred_element_type=F32)
        found = found + lax.dot_general(low, pick, dims, preferred_element_type=F32)
        obs_ref[pl.ds(member, 1), :] = jnp.sum(jnp.where(pick_y, found, 0.0), axis=0, keepdims=True)


def forecast(state, low, high, speed_x, speed_y, diffuse, obs_cell, share):
    memb_dev, levels, width_x, width_y = state.shape
    fields = memb_dev * levels
    groups = width_x // share
    return pl.pallas_call(
        functools.partial(forecast_kernel, share),
        out_shape=[
            jax.ShapeDtypeStruct((groups, memb_dev, share * levels, width_y), F32),
            jax.ShapeDtypeStruct((memb_dev, obs_cell.shape[0]), F32),
        ],
        scratch_shapes=[
            pltpu.VMEM((fields + 2 * levels + 1, width_x + 2 * STEPS, width_y), F32),
            pltpu.VMEM((memb_dev, levels * width_x, width_y), F32),
        ],
        name="forecast",
    )(state.reshape(fields, width_x, width_y), low, high, speed_x, speed_y, diffuse, obs_cell.reshape(1, -1))


def weight_kernel(place_ref, info_ref, list_ref, count_ref, weight_ref):
    domains, slots = list_ref.shape
    obs = info_ref.shape[2]
    limit = float((8 * LOC) ** 2)
    slot = lax.broadcasted_iota(jnp.int32, (domains, slots), 1)
    last = jnp.sum(
        jnp.where(slot == count_ref[...] - 1, list_ref[...], 0).astype(F32), axis=1, keepdims=True
    )
    centre_x = place_ref[0].astype(F32)
    centre_y = lax.broadcasted_iota(jnp.int32, (domains, 1), 0).astype(F32) * (2.0 * DB) + (DB - 1.0)

    def distance(tile):
        delta_x = 2.0 * info_ref[tile, 0:1, :] - centre_x
        delta_y = 2.0 * info_ref[tile, 1:2, :] - centre_y
        return delta_x * delta_x + delta_y * delta_y

    def score_of(tile, dist):
        inside = jnp.minimum(dist, limit)
        if tile == 0:
            inside = jnp.where(place_ref[1] > 0, inside, limit)
        if tile == 2:
            inside = jnp.where(place_ref[2] > 0, inside, limit)
        column = lax.broadcasted_iota(jnp.int32, (1, obs), 1).astype(F32) + float(tile * obs)
        return inside * float(3 * obs) + column, column

    bound = jnp.zeros((domains, 1), F32)
    for tile in range(3):
        score, column = score_of(tile, distance(tile))
        bound = bound + jnp.sum(jnp.where(column == last, score, 0.0), axis=1, keepdims=True)
    for tile in range(3):
        dist = distance(tile)
        score, _ = score_of(tile, dist)
        weight = info_ref[tile, 3:4, :] * jnp.exp(dist * (-1.0 / (8.0 * LOC * LOC)))
        high, low = split_2(jnp.where(score <= bound, weight, 0.0))
        weight_ref[0:domains, pl.ds(tile * obs, obs)] = high
        weight_ref[domains : 2 * domains, pl.ds(tile * obs, obs)] = low


def weights(place, info, lists, counts):
    domains = lists.shape[0]
    vmem = pl.BlockSpec(memory_space=pltpu.VMEM)
    return pl.pallas_call(
        weight_kernel,
        in_specs=[pl.BlockSpec(memory_space=pltpu.SMEM), vmem, vmem, vmem],
        out_specs=vmem,
        out_shape=jax.ShapeDtypeStruct((2 * domains, 3 * info.shape[2]), BF16),
        name="weights",
    )(place, info, lists, counts)


def pair_rows(members):
    half = 2 * SUB
    starts = [half * (k // half) for k in range(members)]
    offsets, total = [], 0
    for start in starts:
        offsets.append(total)
        total += members - start
    return starts, offsets, total


def transform_kernel(ens_ref, info_ref, weight_ref, inv_ref, mean_ref, y_ref, zh_ref, zl_ref, gram_ref, low_ref, s_ref):
    groups, triple, obs = ens_ref.shape
    memb_dev = triple // 3
    members = groups * memb_dev
    starts, offsets, total = pair_rows(members)
    sums = None
    for tile in range(3):
        for group in range(groups):
            y_ref[pl.ds(group * memb_dev, memb_dev), :] = ens_ref[group, pl.ds(tile * memb_dev, memb_dev), :]
        ens = y_ref[...]
        ens_mean = jnp.mean(ens, axis=0, keepdims=True)
        y = ens - ens_mean
        y_ref[...] = y
        for k in range(members):
            prod = y[starts[k] :, :] * y_ref[pl.ds(k, 1), :]
            high, low = split_2(prod)
            zh_ref[pl.ds(offsets[k], members - starts[k]), :] = high
            zl_ref[pl.ds(offsets[k], members - starts[k]), :] = low
        high, low = split_2(y * (info_ref[tile, 2:3, :] - ens_mean))
        zh_ref[pl.ds(total, members), :] = high
        zl_ref[pl.ds(total, members), :] = low
        dims = (((1,), (1,)), ((), ()))
        weight = weight_ref[:, pl.ds(tile * obs, obs)]
        part = lax.dot_general(zh_ref[...], weight, dims, preferred_element_type=F32)
        part = part + lax.dot_general(zl_ref[...], weight, dims, preferred_element_type=F32)
        sums = part if sums is None else sums + part

    width = sums.shape[1]
    domain = lax.broadcasted_iota(jnp.int32, (width, LANES), 0) % (width // 2)
    column = lax.broadcasted_iota(jnp.int32, (width, LANES), 1) // DB
    spread = (domain == column).astype(F32).astype(BF16)
    high, low = split_2(sums)
    rest = (sums - high.astype(F32) - low.astype(F32)).astype(BF16)
    gram = jnp.dot(high, spread, preferred_element_type=F32)
    gram = gram + jnp.dot(low, spread, preferred_element_type=F32)
    gram = gram + jnp.dot(rest, spread, preferred_element_type=F32)
    gram_ref[...] = gram

    sub_row = lax.broadcasted_iota(jnp.int32, (SUB, LANES), 0)

    def every(ref, row):
        return ref[pl.ds(row, SUB, stride=0), :]

    blocks = members // SUB
    mean = [jnp.zeros((SUB, LANES), F32) for _ in range(blocks)]
    for k in range(members):
        own = k // SUB
        acc = [gram_ref[pl.ds(offsets[k] - starts[k] + b * SUB, SUB), :] for b in range(own, blocks)]
        acc[0] = acc[0] + jnp.where(sub_row == k % SUB, members - 1.0, 0.0)
        inv = [jnp.zeros((SUB, LANES), F32) for _ in range(own)]
        inv.append(jnp.where(sub_row == k % SUB, 1.0, 0.0))
        forced = every(gram_ref, total + k)
        for j in range(k):
            base = offsets[j] - starts[j]
            factor = every(low_ref, base + k)
            for b in range(own, blocks):
                acc[b - own] = acc[b - own] - low_ref[pl.ds(base + b * SUB, SUB), :] * factor
            for b in range(j // SUB + 1):
                inv[b] = inv[b] - inv_ref[j, pl.ds(b * SUB, SUB), :] * factor
            forced = forced - s_ref[j] * factor
        pivot = jnp.broadcast_to(acc[0][k % SUB : k % SUB + 1, :], (SUB, LANES))
        scale = lax.rsqrt(pivot)
        scale = scale * (1.5 - 0.5 * pivot * scale * scale)
        for b in range(own, blocks):
            low_ref[pl.ds(offsets[k] - starts[k] + b * SUB, SUB), :] = acc[b - own] * scale
        forced = forced * scale
        s_ref[k] = forced
        for b in range(own + 1):
            inv[b] = inv[b] * scale
            inv_ref[k, pl.ds(b * SUB, SUB), :] = inv[b]
            mean[b] = mean[b] + inv[b] * forced
    for b in range(blocks):
        mean_ref[pl.ds(b * SUB, SUB), :] = mean[b]


def transforms(ens, info, weight):
    groups, triple, obs = ens.shape
    members = groups * triple // 3
    _, _, total = pair_rows(members)
    return pl.pallas_call(
        transform_kernel,
        out_shape=[
            jax.ShapeDtypeStruct((members, members, LANES), F32),
            jax.ShapeDtypeStruct((members, LANES), F32),
        ],
        scratch_shapes=[
            pltpu.VMEM((members, obs), F32),
            pltpu.VMEM((total + members, obs), BF16),
            pltpu.VMEM((total + members, obs), BF16),
            pltpu.VMEM((total + members, LANES), F32),
            pltpu.VMEM((total, LANES), F32),
            pltpu.VMEM((members, SUB, LANES), F32),
        ],
        name="transform",
    )(ens, info, weight)


def apply_kernel(field_ref, inv_ref, mean_ref, out_ref):
    groups, memb_dev, rows, _ = field_ref.shape
    members = groups * memb_dev
    root = float(members - 1) ** 0.5

    @pl.loop(0, rows // SUB)
    def _(block):
        at = pl.ds(pl.multiple_of(block * SUB, SUB), SUB)
        fields = [field_ref[j // memb_dev, j % memb_dev, at, :] for j in range(members)]
        total = fields[0]
        for j in range(1, members):
            total = total + fields[j]
        mean = total * (1.0 / members)
        fields = [field - mean for field in fields]
        base = mean
        for j in range(members):
            base = base + fields[j] * mean_ref[pl.ds(j, SUB, stride=0), :]
        for k in range(members):
            acc = fields[0] * inv_ref[k, pl.ds(0, SUB, stride=0), :]
            for j in range(1, k + 1):
                acc = acc + fields[j] * inv_ref[k, pl.ds(j, SUB, stride=0), :]
            out_ref[k // memb_dev, k % memb_dev, at, :] = base + root * acc


def apply_transform(fields, inverse, mean):
    return pl.pallas_call(
        apply_kernel,
        out_shape=jax.ShapeDtypeStruct(fields.shape, F32),
        name="apply",
    )(fields, inverse, mean)


def unpack_kernel(share, in_ref, out_ref):
    groups, memb_dev, rows, _ = in_ref.shape
    levels = rows // share
    width_x = groups * share
    for group in range(groups):
        for member in range(memb_dev):
            for row in range(share):
                out_ref[member, pl.ds(group * share + row, levels, stride=width_x), :] = in_ref[
                    group, member, pl.ds(row * levels, levels), :
                ]


def unpack(parts, share):
    groups, memb_dev, rows, width_y = parts.shape
    return pl.pallas_call(
        functools.partial(unpack_kernel, share),
        out_shape=jax.ShapeDtypeStruct((memb_dev, groups * rows, width_y), F32),
        name="unpack",
    )(parts)


def neighbours(low, high):
    count = lax.axis_size("tile")
    up = [(i, i + 1) for i in range(count - 1)]
    down = [(i + 1, i) for i in range(count - 1)]
    return lax.ppermute(high, "tile", up), lax.ppermute(low, "tile", down)


def local(state, speed_x, speed_y, diffuse, obs_cell, obs_value, obs_errinv, obs_list, obs_count):
    memb_dev, levels, width_x, width_y = state.shape
    groups = lax.axis_size(GROUP)
    tiles = lax.axis_size("tile")
    tile_index = lax.axis_index("tile")
    group_idx = lax.axis_index(GROUP)
    share = width_x // groups
    obs = obs_cell.shape[0]

    low, high = pack(state, speed_x, speed_y, diffuse)
    low, high = neighbours(low, high)
    fields, own_obs = forecast(state, low, high, speed_x, speed_y, diffuse, obs_cell, share)
    received = lax.all_to_all(fields, GROUP, 0, 0, tiled=True)

    global_x = (tile_index * width_x + obs_cell // width_y % width_x).astype(F32)
    local_y = (obs_cell % width_y).astype(F32)
    rows = jnp.concatenate(
        [own_obs, jnp.stack([global_x, local_y, obs_value, obs_errinv])], axis=0
    )
    below, above = neighbours(rows, rows)
    window = jnp.stack([below, rows, above])
    info = window[:, memb_dev:]
    ens = window[:, :memb_dev].reshape(1, 3 * memb_dev, obs)
    ens = lax.all_to_all(
        jnp.broadcast_to(ens, (groups, 3 * memb_dev, obs)), GROUP, 0, 0, tiled=True
    )

    share_d = share // DB
    lists = lax.dynamic_slice_in_dim(obs_list, group_idx * share_d, share_d, 0).reshape(-1, obs_list.shape[2])
    counts = lax.dynamic_slice_in_dim(obs_count, group_idx * share_d, share_d, 0).reshape(-1, 1)
    place = jnp.stack(
        [
            2 * (tile_index * width_x + group_idx * share) + DB - 1,
            (tile_index > 0).astype(jnp.int32),
            (tile_index < tiles - 1).astype(jnp.int32),
        ]
    )
    weight = weights(place, info, lists, counts)
    inverse, mean = transforms(ens, info, weight)
    analysed = apply_transform(received, inverse, mean)
    back = lax.all_to_all(analysed, GROUP, 0, 0, tiled=True)
    return unpack(back, share).reshape(state.shape)


def solution(mesh):
    placed = (
        P(GROUP, None, "tile", None),
        P(None, "tile", None),
        P(None, "tile", None),
        P("tile", None),
        P("tile"),
        P("tile"),
        P("tile"),
        P("tile", None, None),
        P("tile", None),
    )
    return jax.shard_map(
        local,
        mesh=mesh,
        in_specs=placed,
        out_specs=P(GROUP, None, "tile", None),
        check_vma=False,
    )
```

time: 399 us -> 82.2 us (0.21)
  other arithmetic: 210 us -> 0.64 us
  local copies, waits for them, and re-layouts: 90.2 us -> 6.34 us
  Pallas kernels: 0 us -> 24.2 us
  matrix products: 17.8 us -> 0 us
  starting transfers between devices: 25.9 us -> 15.6 us
  waiting for transfers between devices: 18.3 us -> 8.11 us
  blocking collectives: 35.5 us -> 26.5 us
    another operation x6 -> x2, other arithmetic: 201 us -> 0.62 us  [the longest x1 0.61 us: local(): jnp.stack([2 * (tile_index * width_x + group_idx * share) + DB - 1, (tile...]
    gather x3 -> x0, local copies, waits for them, and re-layouts: 68.3 us -> none  [the longest x2 59.7 us: analyze(): chosen = window[:, flat_lists]]
    pallas_call x0 -> x6, Pallas kernels: none -> 24.2 us  [the longest x1 8.63 us: forecast(): pl.pallas_call(functools.partial(forecast_kernel, share), out_shape=[jax....]
    all_gather x1 -> x0, blocking collectives: 23.5 us -> none  [local(): all_ens = lax.all_gather(own_ens, ('section', 'mem'), axis=0, tiled=True)]
    all_to_all x1 -> x2, blocking collectives: 12 us -> 26.5 us  [the longest x1 13.5 us: local(): back = lax.all_to_all(analysed, GROUP, 0, 0, tiled=True)]
    dot_general x3 -> x0, matrix products: 13.9 us -> none  [the longest x1 8.71 us: analyze(): jnp.einsum('jlaxcy,acjk->klaxcy', anomaly, trans_grid, precision=lax.Prec...]
    ppermute x10 -> x4, waiting for transfers between devices: 18.3 us -> 8.11 us  [neighbours(): return (lax.ppermute(high, 'tile', up), lax.ppermute(low, 'tile', down))]
    ppermute x10 -> x4, starting transfers between devices: 22.2 us -> 12.1 us  [neighbours(): return (lax.ppermute(high, 'tile', up), lax.ppermute(low, 'tile', down))]
  transfers between devices with their start and end apart: 11 -> 5, of which waited for: 8 -> 3; matrix products, arithmetic and copies ran while one was open for 70% -> 3% of each run, Pallas kernels for 0% -> 11%
where the time goes in v1:
time: 82.2 us; the launch traced here: 81.5 us
  blocking collectives  26.5 us (32%)
  Pallas kernels  24.2 us (29%)
  starting transfers between devices  15.6 us (19%)
  waiting for transfers between devices  8.11 us (10%)
  local copies, waits for them, and re-layouts  6.34 us (8%)
    all_to_all x1, blocking collectives, local(): back = lax.all_to_all(analysed, GROUP, 0, 0, tiled=True)  13.5 us
    all_to_all x1, blocking collectives, local(): lax.all_to_all(jnp.broadcast_to(ens, (groups, 3 * memb_dev, obs)), GROUP,...  13 us
    ppermute x4, starting transfers between devices, neighbours(): return (lax.ppermute(high, 'tile', up), lax.ppermute(low, 'tile', down))  12.1 us
    pallas_call x1, Pallas kernels, forecast(): pl.pallas_call(functools.partial(forecast_kernel, share), out_shape=[jax....  8.63 us
    ppermute x4, waiting for transfers between devices, neighbours(): return (lax.ppermute(high, 'tile', up), lax.ppermute(low, 'tile', down))  8.11 us
    pallas_call x1, Pallas kernels, transforms(): pl.pallas_call(transform_kernel, out_shape=[jax.ShapeDtypeStruct((members...  6.13 us
    all_to_all x1, starting transfers between devices, local(): received = lax.all_to_all(fields, GROUP, 0, 0, tiled=True)  3.49 us
    unnamed x14, local copies, waits for them, and re-layouts  2.86 us
  transfers between devices with their start and end apart: 5, of which 3 were waited for; matrix products, arithmetic and copies ran while one was open for 3% of the time, Pallas kernels for 11%

profile of v1, /device:TPU:0, one launch (start us, length us, event | category | flops | bytes accessed | tf_op | source)
XLA Modules:
  0.0 81.5 jit_solution(1256630035156019278)
XLA Ops:
  0.0 0.0 copy-start
  0.0 2.0 %pack.1 = (f32[392,128]{1,0:T(8,128)}, f32[392,128]{1,0:T(8,128)}) custom-call(f32[64,16,128]{2,1,0:T(8,128)} %bitcast.17, f32[16,16,128]{2,1,0:T(8,128)} %sx_ref.3, f32[16,16,128]{2,1,0:T(8,128)} %sy_ref.3, f32[16,128]{1,0:T(8,128)} %diff_ref.3), custom_call_target="tpu_custom_call" | custom-call | tf_op jit(solution)/shard_map/pack/pallas_call | solution.py:42
  2.0 5.0 %collective-permute-start = (f32[392,128]{1,0:T(8,128)}, f32[392,128]{1,0:T(8,128)S(1)}, u32[]{:S(2)}, u32[]{:S(2)}) collective-permute-start(f32[392,128]{1,0:T(8,128)} %get-tuple-element.11), channel_id=1, source_target_pairs={{0,4},{4,8},{8,12},{1,5},{5,9},{9,13},{2,6},{6,10},{10,14},{3,7},{... | collective-permute-start | bytes 602120 | tf_op jit(solution)/shard_map/ppermute | solution.py:350
  7.0 1.3 %collective-permute-start.1 = (f32[392,128]{1,0:T(8,128)}, f32[392,128]{1,0:T(8,128)S(1)}, u32[]{:S(2)}, u32[]{:S(2)}) collective-permute-start(f32[392,128]{1,0:T(8,128)} %get-tuple-element.12), channel_id=1, source_target_pairs={{4,0},{8,4},{12,8},{5,1},{9,5},{13,9},{6,2},{10,6},{14,10},{7,3},{... | collective-permute-start | bytes 602120 | tf_op jit(solution)/shard_map/ppermute | solution.py:350
  8.3 0.0 copy-start.4
  8.3 0.7 copy-done.4
  9.0 2.5 %collective-permute-done.low_ref = f32[392,128]{1,0:T(8,128)S(1)} collective-permute-done((f32[392,128]{1,0:T(8,128)}, f32[392,128]{1,0:T(8,128)S(1)}, u32[]{:S(2)}, u32[]{:S(2)}) %collective-permute-start) | collective-permute-done | bytes 200736 | tf_op jit(solution)/shard_map/ppermute | solution.py:350
  11.5 0.0 copy-start.2
  11.5 4.0 %collective-permute-done.1.high_ref = f32[392,128]{1,0:T(8,128)S(1)} collective-permute-done((f32[392,128]{1,0:T(8,128)}, f32[392,128]{1,0:T(8,128)S(1)}, u32[]{:S(2)}, u32[]{:S(2)}) %collective-permute-start.1) | collective-permute-done | bytes 200736 | tf_op jit(solution)/shard_map/ppermute | solution.py:350
  15.5 0.0 copy-start.3
  15.5 0.0 copy-done.2
  15.5 0.7 copy-done.3
  16.2 8.6 %forecast.1 = (f32[8,4,32,128]{3,2,1,0:T(8,128)}, f32[4,1024]{1,0:T(4,128)}) custom-call(f32[64,16,128]{2,1,0:T(8,128)} %bitcast.18, f32[392,128]{1,0:T(8,128)} %copy-done.2, f32[392,128]{1,0:T(8,128)} %copy-done.3, f32[16,16,128]{2,1,0:T(8,128)} %sx_ref.3, f32[16,16,128]{2,1,0:T(8,128)} %sy_ref.3, f32[16,128]{1,0:T(8,128)} %diff_ref.3, s32[1,1024]{1,0:T(1,128)} %bitcast.22), custom_call_target="tpu_custom_call" | custom-call | tf_op jit(solution)/shard_map/forecast/pallas_call | solution.py:122
  24.8 0.0 copy-start.6
  24.8 0.0 copy-start.5
  24.8 0.7 copy-done.6
  25.5 0.0 copy-done.5
  25.5 0.8 concatenate.3
  26.3 1.3 %collective-permute-start.3 = (f32[8,1024]{1,0:T(8,128)S(1)}, f32[8,1024]{1,0:T(8,128)S(1)}, u32[]{:S(2)}, u32[]{:S(2)}) collective-permute-start(f32[8,1024]{1,0:T(8,128)S(1)} %concatenate.3), channel_id=1, source_target_pairs={{4,0},{8,4},{12,8},{5,1},{9,5},{13,9},{6,2},{10,6},{14,10},{7,3},{... | collective-permute-start | bytes 98312 | tf_op jit(solution)/shard_map/ppermute | solution.py:350
  27.6 4.5 %collective-permute-start.2 = (f32[8,1024]{1,0:T(8,128)S(1)}, f32[8,1024]{1,0:T(8,128)S(1)}, u32[]{:S(2)}, u32[]{:S(2)}) collective-permute-start(f32[8,1024]{1,0:T(8,128)S(1)} %concatenate.3), channel_id=1, source_target_pairs={{0,4},{4,8},{8,12},{1,5},{5,9},{9,13},{2,6},{6,10},{10,14},{3,7},{... | collective-permute-start | bytes 98312 | tf_op jit(solution)/shard_map/ppermute | solution.py:350
  32.2 0.0 collective-permute-done.3
  32.2 1.6 %collective-permute-done.2 = f32[8,1024]{1,0:T(8,128)S(1)} collective-permute-done((f32[8,1024]{1,0:T(8,128)S(1)}, f32[8,1024]{1,0:T(8,128)S(1)}, u32[]{:S(2)}, u32[]{:S(2)}) %collective-permute-start.2) | collective-permute-done | bytes 32800 | tf_op jit(solution)/shard_map/ppermute | solution.py:350
  33.7 0.6 fusion.6
  34.5 13.0 %all_to_all.15.ens_ref = f32[8,12,1024]{2,1,0:T(8,128)} all-to-all(f32[8,12,1024]{2,1,0:T(8,128)S(1)} %broadcast_in_dim.8), channel_id=1, replica_groups=mesh['section'=2,'tile'=4,'mem'=4] {'section','mem'}, dimensions={0} | all-to-all | bytes 786432 | tf_op jit(solution)/shard_map/all_to_all | solution.py:376
  47.4 3.5 %all-to-all-start = ((f32[8,4,32,128]{3,2,1,0:T(8,128)}), f32[8,4,32,128]{3,2,1,0:T(8,128)S(1)}, u32[]{:S(2)}, u32[]{:S(2)}) async-start(f32[8,4,32,128]{3,2,1,0:T(8,128)} %get-tuple-element.13), calls=%async_computation | async-start | bytes 1048576 | tf_op jit(solution)/shard_map/all_to_all | solution.py:365
  51.0 0.7 dynamic-slice_bitcast_fusion.1
  51.7 0.7 copy.10.count_ref
  52.4 0.6 pad_add_fusion.place_ref
  53.0 0.0 copy-done
  53.0 0.6 dynamic-slice_bitcast_fusion.list_ref
  53.6 2.5 %weights.1.weight_ref = bf16[128,3072]{1,0:T(8,128)(2,1)} custom-call(s32[3]{0:T(128)} %pad_add_fusion.place_ref, f32[3,4,1024]{2,1,0:T(4,128)} %get-tuple-element.17.info_ref, s32[64,256]{1,0:T(8,128)} %dynamic-slice_bitcast_fusion.list_ref, s32[64,1]{1,0:T(8,128)} %copy.10.count_ref), custom_call_target="tpu_custom_call" | custom-call | tf_op jit(solution)/shard_map/weights/pallas_call | solution.py:177
  56.1 6.1 %transform.1 = (f32[32,32,128]{2,1,0:T(8,128)}, f32[32,128]{1,0:T(8,128)}) custom-call(f32[8,12,1024]{2,1,0:T(8,128)} %all_to_all.15.ens_ref, f32[3,4,1024]{2,1,0:T(4,128)} %get-tuple-element.17.info_ref, bf16[128,3072]{1,0:T(8,128)(2,1)} %weights.1.weight_ref), custom_call_target="tpu_custom_call" | custom-call | tf_op jit(solution)/shard_map/transform/pallas_call | solution.py:275
  62.3 0.0 all-to-all-done.field_ref
  62.3 0.0 copy-start.1
  62.3 0.8 copy-done.1
  63.1 2.8 %apply.1 = f32[8,4,32,128]{3,2,1,0:T(8,128)} custom-call(f32[8,4,32,128]{3,2,1,0:T(8,128)} %copy-done.1, f32[32,32,128]{2,1,0:T(8,128)} %get-tuple-element.15.inv_ref, f32[32,128]{1,0:T(8,128)} %get-tuple-element.16.mean_ref), custom_call_target="tpu_custom_call" | custom-call | tf_op jit(solution)/shard_map/apply/pallas_call | solution.py:318
  65.9 13.5 %all_to_all.16.in_ref = f32[8,4,32,128]{3,2,1,0:T(8,128)} all-to-all(f32[8,4,32,128]{3,2,1,0:T(8,128)} %apply.1), channel_id=1, replica_groups=mesh['section'=2,'tile'=4,'mem'=4] {'section','mem'}, dimensions={0} | all-to-all | bytes 1048576 | tf_op jit(solution)/shard_map/all_to_all | solution.py:393
  79.4 2.0 %unpack.1 = f32[4,256,128]{2,1,0:T(8,128)} custom-call(f32[8,4,32,128]{3,2,1,0:T(8,128)} %all_to_all.16.in_ref), custom_call_target="tpu_custom_call" | custom-call | tf_op jit(solution)/shard_map/unpack/pallas_call | solution.py:339
  (4 shorter events, 0.1 us)
Async XLA Ops:
  0.0 53.0 %copy-start = (s32[8,64,256]{2,1,0:T(8,128)S(1)}, s32[8,64,256]{2,1,0:T(8,128)}, u32[]{:S(2)}) copy-start(s32[8,64,256]{2,1,0:T(8,128)} %param.16) | copy-start | bytes 1572868
  2.0 9.5 %collective-permute-start = (f32[392,128]{1,0:T(8,128)}, f32[392,128]{1,0:T(8,128)S(1)}, u32[]{:S(2)}, u32[]{:S(2)}) collective-permute-start(f32[392,128]{1,0:T(8,128)} %get-tuple-element.11), channel_id=1, source_target_pairs={{0,4},{4,8},{8,12},{1,5},{5,9},{9,13},{2,6},{6,10},{10,14},{3,7},{... | collective-permute-start | bytes 602120 | tf_op jit(solution)/shard_map/ppermute | solution.py:350
  7.0 8.6 %collective-permute-start.1 = (f32[392,128]{1,0:T(8,128)}, f32[392,128]{1,0:T(8,128)S(1)}, u32[]{:S(2)}, u32[]{:S(2)}) collective-permute-start(f32[392,128]{1,0:T(8,128)} %get-tuple-element.12), channel_id=1, source_target_pairs={{4,0},{8,4},{12,8},{5,1},{9,5},{13,9},{6,2},{10,6},{14,10},{7,3},{... | collective-permute-start | bytes 602120 | tf_op jit(solution)/shard_map/ppermute | solution.py:350
  8.3 0.7 copy-start.4
  11.5 4.0 %copy-start.2 = (f32[392,128]{1,0:T(8,128)}, f32[392,128]{1,0:T(8,128)S(1)}, u32[]{:S(2)}) copy-start(f32[392,128]{1,0:T(8,128)S(1)} %collective-permute-done.low_ref) | copy-start | bytes 602116
  15.5 0.7 copy-start.3
  24.8 0.7 copy-start.6
  24.8 0.7 copy-start.5
  26.3 5.9 %collective-permute-start.3 = (f32[8,1024]{1,0:T(8,128)S(1)}, f32[8,1024]{1,0:T(8,128)S(1)}, u32[]{:S(2)}, u32[]{:S(2)}) collective-permute-start(f32[8,1024]{1,0:T(8,128)S(1)} %concatenate.3), channel_id=1, source_target_pairs={{4,0},{8,4},{12,8},{5,1},{9,5},{13,9},{6,2},{10,6},{14,10},{7,3},{... | collective-permute-start | bytes 98312 | tf_op jit(solution)/shard_map/ppermute | solution.py:350
  27.6 6.1 %collective-permute-start.2 = (f32[8,1024]{1,0:T(8,128)S(1)}, f32[8,1024]{1,0:T(8,128)S(1)}, u32[]{:S(2)}, u32[]{:S(2)}) collective-permute-start(f32[8,1024]{1,0:T(8,128)S(1)} %concatenate.3), channel_id=1, source_target_pairs={{0,4},{4,8},{8,12},{1,5},{5,9},{9,13},{2,6},{6,10},{10,14},{3,7},{... | collective-permute-start | bytes 98312 | tf_op jit(solution)/shard_map/ppermute | solution.py:350
  47.4 14.8 %all-to-all-start = ((f32[8,4,32,128]{3,2,1,0:T(8,128)}), f32[8,4,32,128]{3,2,1,0:T(8,128)S(1)}, u32[]{:S(2)}, u32[]{:S(2)}) async-start(f32[8,4,32,128]{3,2,1,0:T(8,128)} %get-tuple-element.13), calls=%async_computation | async-start | bytes 1048576 | tf_op jit(solution)/shard_map/all_to_all | solution.py:365
  62.3 0.8 copy-start.1
